TPU v7x, 32 devices: a whole 2x2x4 slice. The times are simulated.
32 devices in a mesh: ctx: 8 (over z, y), tp: 4 (over x, core).
Axes of the slice: x: 2, y: 2, z: 4, core: 2. Of those that a mesh axis runs over, the one named last changes fastest.
Arguments:
- qkv: bfloat16 [1024, 3, 8192], P(('ctx', 'tp')), may hold values from -6 to 6
- filters: float32 [3, 7, 8192], P(None, None, 'tp'), may hold values from -1.5 to 1.5
- doc_ids: int32 [8], replicated, may hold values from 0 to 1, never falling along the last dimension, each value on 1 to 5 neighbouring positions
- upstream: bfloat16 [1024, 8192], P('ctx', 'tp'), may hold values from -6 to 6
Outputs:
- attended: bfloat16 [1024, 8192], P('ctx', 'tp')
- qkv_grad: bfloat16 [1024, 3, 8192], P(('ctx', 'tp'))
- filter_grad: float32 [3, 7, 8192], P(None, None, 'tp')
Inputs may be any that keep to these rules, and one draw needn't show every extreme that they name: doc_ids never falls along the sequence; every document covers 1 to 5 whole blocks of 128 tokens.
All inputs are finite; a program needn't handle non-finite values.
Results may differ from a plain program's by a relative error of at most 0.014.
The roundings to bfloat16 on the way count: a program that leaves them out, or rounds other values in their place, can miss the bound.
Values may be sent and summed in bfloat16 or wider, within the bound.
No kernel may reach another device: no remote copies, remote signals or barrier semaphores. Data moves between devices by JAX's collectives and lax.ppermute only.
A program may use at most 128 MiB of HBM per device.

v0:
```python
import jax
import jax.numpy as jnp
from jax import lax
from jax.sharding import PartitionSpec as P

HEAD_DIM = 128
KW = 7
BLOCK = 128
STEPS = 4


def from_behind(value, axis, steps):
    count = lax.axis_size(axis)
    first, last = (max(0, -steps), min(count, count - steps))
    return lax.ppermute(value, axis, [(source, source + steps) for source in range(first, last)])


def block_docs(doc_ids, first_block, count):
    start = jnp.maximum(first_block, 0)
    picked = lax.dynamic_slice_in_dim(doc_ids, start, count)
    return jnp.repeat(picked, BLOCK)


def shards(qkv, filters, doc_ids, upstream):
    local = lax.all_to_all(qkv, "tp", split_axis=2, concat_axis=0, tiled=True)
    tokens = local.shape[0]
    width = local.shape[2]
    heads = width // HEAD_DIM
    blocks_here = tokens // BLOCK
    logit_scale = HEAD_DIM ** (-0.5)
    position = lax.axis_index("ctx")
    reach = STEPS + 1
    rim = from_behind(local[tokens - (KW - 1) :], "ctx", 1)
    inputs = jnp.concatenate([rim, local], axis=0).astype(jnp.float32)
    mixed = sum(
        (filters[:, lag, :] * inputs[KW - 1 - lag : KW - 1 - lag + tokens] for lag in range(KW))
    )
    mixed = mixed.astype(jnp.bfloat16)
    queries = mixed[:, 0].reshape(tokens, heads, HEAD_DIM)
    key_value = mixed[:, 1:3]
    tiles = [key_value]
    current = key_value
    for distance in range(1, STEPS + 1):
        current = from_behind(current, "ctx", 1)
        tiles.append(current)
    joined = jnp.concatenate(tiles, axis=0)
    keys = joined[:, 0].reshape(reach * tokens, heads, HEAD_DIM)
    values = joined[:, 1].reshape(reach * tokens, heads, HEAD_DIM)
    rows = jnp.arange(tokens)
    query_token = position * tokens + rows
    query_doc = block_docs(doc_ids, position * blocks_here, blocks_here)
    key_tokens = jnp.concatenate(
        [(position - distance) * tokens + rows for distance in range(reach)]
    )
    key_docs = jnp.concatenate(
        [
            block_docs(doc_ids, (position - distance) * blocks_here, blocks_here)
            for distance in range(reach)
        ]
    )
    allowed = (
        (key_tokens[None, :] >= 0)
        & (key_tokens[None, :] <= query_token[:, None])
        & (key_docs[None, :] == query_doc[:, None])
    )
    raw = (
        jnp.einsum("qhd,khd->hqk", queries, keys, preferred_element_type=jnp.float32) * logit_scale
    )
    masked = jnp.where(allowed[None], raw, -1e30)
    row_max = masked.max(axis=2)
    expo = jnp.where(allowed[None], jnp.exp(masked - row_max[:, :, None]), 0.0)
    row_sum = expo.sum(axis=2)
    weighted_values = jnp.einsum(
        "hqk,khd->qhd", expo.astype(jnp.bfloat16), values, preferred_element_type=jnp.float32
    )
    attended = (weighted_values / row_sum.T[:, :, None]).astype(jnp.bfloat16)
    grad_out = upstream.reshape(tokens, heads, HEAD_DIM)
    delta = jnp.sum(grad_out.astype(jnp.float32) * attended.astype(jnp.float32), axis=-1).T
    prob = expo / row_sum[:, :, None]
    value_part = jnp.einsum(
        "hqk,qhd->khd", prob.astype(jnp.bfloat16), grad_out, preferred_element_type=jnp.float32
    )
    probability_gradient = jnp.einsum(
        "qhd,khd->hqk", grad_out, values, preferred_element_type=jnp.float32
    )
    score_gradient = (prob * (probability_gradient - delta[:, :, None]) * logit_scale).astype(
        jnp.bfloat16
    )
    query_gradient_rows = jnp.einsum(
        "hqk,khd->qhd", score_gradient, keys, preferred_element_type=jnp.float32
    )
    key_part = jnp.einsum(
        "hqk,qhd->khd", score_gradient, queries, preferred_element_type=jnp.float32
    )
    stacked = jnp.stack(
        [key_part.reshape(reach, tokens, width), value_part.reshape(reach, tokens, width)], axis=2
    )
    partials = [stacked[distance] for distance in range(reach)]
    carried = partials[STEPS]
    for distance in range(STEPS - 1, -1, -1):
        carried = from_behind(carried, "ctx", -1)
        carried = carried + partials[distance]
    conv_grad = jnp.concatenate([query_gradient_rows.reshape(tokens, 1, width), carried], axis=1)
    grad_edge = from_behind(conv_grad[: KW - 1], "ctx", -1)
    extended = jnp.concatenate([conv_grad, grad_edge], axis=0)
    input_grad = sum((filters[:, lag, :] * extended[lag : lag + tokens] for lag in range(KW)))
    tap_terms = jnp.stack(
        [
            jnp.sum(inputs[KW - 1 - lag : KW - 1 - lag + tokens] * conv_grad, axis=0)
            for lag in range(KW)
        ],
        axis=1,
    )
    filter_grad = lax.psum(tap_terms, "ctx")
    qkv_grad = lax.all_to_all(
        input_grad.astype(jnp.bfloat16), "tp", split_axis=0, concat_axis=2, tiled=True
    )
    return (attended.reshape(tokens, width), qkv_grad, filter_grad)


def solution(mesh):
    return jax.shard_map(
        shards,
        mesh=mesh,
        in_specs=(P(("ctx", "tp"), None, None), P(None, None, "tp"), P(), P("ctx", "tp")),
        out_specs=(P("ctx", "tp"), P(("ctx", "tp"), None, None), P(None, None, "tp")),
        check_vma=False,
    )
```

profile of v0, /device:TPU:0, one launch (start us, length us, event | category | flops | bytes accessed | tf_op | source)
XLA Modules:
  0.0 541.6 jit_solution(776772498163065581)
XLA Ops:
  7.2 10.7 %copy.57 = bf16[32,3,8192]{0,1,2:T(4,128)(2,1)} copy(bf16[32,3,8192]{2,0,1:T(8,128)(2,1)} %param.4) | data formatting | bytes 3145728 | tf_op args[0]
  17.8 8.4 %reshape.158 = bf16[4,2,98304]{2,1,0:T(2,128)(2,1)} reshape(bf16[8192,3,32]{2,1,0:T(4,128)(2,1)} %bitcast.114) | data formatting | bytes 3145728
  26.2 4.3 all-to-all-start
  30.7 19.9 %all-to-all-done = bf16[4,2,98304]{2,1,0:T(2,128)(2,1)S(1)} async-done(((bf16[4,2,98304]{2,1,0:T(2,128)(2,1)}), bf16[4,2,98304]{2,1,0:T(2,128)(2,1)S(1)}, u32[]{:S(2)}, u32[]{:S(2)}) %all-to-all-start) | async-done | bytes 1572896 | tf_op jit(solution)/shard_map/all_to_all | solution.py:25
  50.6 7.1 %reshape.159 = bf16[8192,3,32]{2,1,0:T(4,128)(2,1)} reshape(bf16[4,2,98304]{2,1,0:T(2,128)(2,1)S(1)} %all-to-all-done) | data formatting | bytes 3145728
  57.7 10.5 %copy.59 = bf16[4,32,3,2048]{3,1,0,2:T(8,128)(2,1)S(1)} copy(bf16[4,32,3,2048]{1,2,3,0:T(4,128)(2,1)} %bitcast.113) | data formatting | bytes 3145728 | tf_op jit(solution)/shard_map/all_to_all | solution.py:25
  68.2 4.2 collective-permute-start
  81.5 5.3 collective-permute-start.1
  86.8 20.0 %collective-permute-done.1 = bf16[128,2,2048]{2,0,1:T(8,128)(2,1)} collective-permute-done((bf16[128,2,2048]{2,0,1:T(8,128)(2,1)S(1)}, bf16[128,2,2048]{2,0,1:T(8,128)(2,1)}, u32[]{:S(2)}, u32[]{:S(2)}) %collective-permute-start.1) | collective-permute-done | bytes 1048608 | tf_op jit(solution)/shard_map/ppermute | solution.py:15
  106.8 5.5 %collective-permute-start.2 = (bf16[128,2,2048]{2,0,1:T(8,128)(2,1)}, bf16[128,2,2048]{2,0,1:T(8,128)(2,1)}, u32[]{:S(2)}, u32[]{:S(2)}) collective-permute-start(bf16[128,2,2048]{2,0,1:T(8,128)(2,1)} %collective-permute-done.1), channel_id=1, source_target_pairs={{0,4},{4,8},{8,12},{12,16},{16,20},{20,24},{24,28},{1,5},{5,9},{9,... | collective-permute-start | bytes 3145736 | tf_op jit(solution)/shard_map/ppermute | solution.py:15
  112.8 19.0 %collective-permute-done.2 = bf16[128,2,2048]{2,0,1:T(8,128)(2,1)} collective-permute-done((bf16[128,2,2048]{2,0,1:T(8,128)(2,1)}, bf16[128,2,2048]{2,0,1:T(8,128)(2,1)}, u32[]{:S(2)}, u32[]{:S(2)}) %collective-permute-start.2) | collective-permute-done | bytes 1048608 | tf_op jit(solution)/shard_map/ppermute | solution.py:15
  131.8 6.2 %collective-permute-start.3 = (bf16[128,2,2048]{2,0,1:T(8,128)(2,1)}, bf16[128,2,2048]{2,0,1:T(8,128)(2,1)}, u32[]{:S(2)}, u32[]{:S(2)}) collective-permute-start(bf16[128,2,2048]{2,0,1:T(8,128)(2,1)} %collective-permute-done.2), channel_id=1, source_target_pairs={{0,4},{4,8},{8,12},{12,16},{16,20},{20,24},{24,28},{1,5},{5,9},{9,... | collective-permute-start | bytes 3145736 | tf_op jit(solution)/shard_map/ppermute | solution.py:15
  141.8 14.7 %collective-permute-done.3 = bf16[128,2,2048]{2,0,1:T(8,128)(2,1)} collective-permute-done((bf16[128,2,2048]{2,0,1:T(8,128)(2,1)}, bf16[128,2,2048]{2,0,1:T(8,128)(2,1)}, u32[]{:S(2)}, u32[]{:S(2)}) %collective-permute-start.3) | collective-permute-done | bytes 1048608 | tf_op jit(solution)/shard_map/ppermute | solution.py:15
  156.5 6.3 %collective-permute-start.4 = (bf16[128,2,2048]{2,0,1:T(8,128)(2,1)}, bf16[128,2,2048]{2,0,1:T(8,128)(2,1)}, u32[]{:S(2)}, u32[]{:S(2)}) collective-permute-start(bf16[128,2,2048]{2,0,1:T(8,128)(2,1)} %collective-permute-done.3), channel_id=1, source_target_pairs={{0,4},{4,8},{8,12},{12,16},{16,20},{20,24},{24,28},{1,5},{5,9},{9,... | collective-permute-start | bytes 3145736 | tf_op jit(solution)/shard_map/ppermute | solution.py:15
  182.7 5.7 %fusion.48 = (bf16[640,1,2048]{2,0,1:T(8,128)(2,1)}, bf16[640,1,2048]{2,0,1:T(8,128)(2,1)}) fusion(bf16[640,2,2048]{2,0,1:T(8,128)(2,1)} %constant_dynamic-update-slice_fusion), kind=kLoop, calls=%fused_computation.106 | loop fusion | bytes 10485760 | tf_op jit(solution)/shard_map/slice | solution.py:47
  188.4 4.4 copy.62
  192.8 4.5 copy.60
  197.2 6.6 %fusion.52 = (f32[16,128]{1,0:T(8,128)S(1)}, f32[16,128,640]{2,1,0:T(8,128)}) fusion(pred[128,640]{1,0:T(8,128)(4,1)} %and_and_fusion, bf16[128,16,128]{0,2,1:T(8,128)(2,1)} %bitcast.124, bf16[640,16,128]{0,2,1:T(8,128)(2,1)} %bitcast.115), kind=kOutput, calls=%fused_computation.110 | convolution fusion | flops 342098560 | bytes 8478720 | tf_op jit(solution)/shard_map/sub | solution.py:71
  203.8 4.1 fusion.18
  213.3 5.3 copy.72
  218.6 6.8 %stack_reshape.7 = f32[5,128,1,2048]{3,1,0,2:T(8,128)} reshape(f32[640,16,128]{2,1,0:T(8,128)} %copy.72) | data formatting | bytes 10485760 | tf_op jit(solution)/shard_map/stack;reshape | solution.py:95
  225.4 5.0 convolution_bitcast_fusion
  230.5 7.4 %reshape.152 = f32[5,128,1,2048]{1,0,3,2:T(8,128)} reshape(f32[640,16,128]{0,2,1:T(8,128)} %convolution_bitcast_fusion) | data formatting | bytes 10485760 | tf_op jit(solution)/shard_map/stack;reshape | solution.py:95
  237.8 7.9 %copy.73 = f32[5,128,1,2048]{3,1,2,0:T(8,128)} copy(f32[5,128,1,2048]{1,0,3,2:T(8,128)} %reshape.152) | data formatting | bytes 10485760 | tf_op jit(solution)/shard_map/stack;reshape | solution.py:95
  249.1 44.7 %collective-permute-done.5 = f32[128,2,2048]{2,0,1:T(8,128)S(1)} collective-permute-done((f32[128,2,2048]{2,0,1:T(8,128)S(1)}, f32[128,2,2048]{2,0,1:T(8,128)S(1)}, u32[]{:S(2)}, u32[]{:S(2)}) %collective-permute-start.5) | collective-permute-done | bytes 2097184 | tf_op jit(solution)/shard_map/ppermute | solution.py:15
  295.7 44.1 %collective-permute-done.6 = f32[128,2,2048]{2,0,1:T(8,128)S(1)} collective-permute-done((f32[128,2,2048]{2,0,1:T(8,128)S(1)}, f32[128,2,2048]{2,0,1:T(8,128)S(1)}, u32[]{:S(2)}, u32[]{:S(2)}) %collective-permute-start.6) | collective-permute-done | bytes 2097184 | tf_op jit(solution)/shard_map/ppermute | solution.py:15
  341.7 42.9 %collective-permute-done.7 = f32[128,2,2048]{2,0,1:T(8,128)S(1)} collective-permute-done((f32[128,2,2048]{2,0,1:T(8,128)S(1)}, f32[128,2,2048]{2,0,1:T(8,128)S(1)}, u32[]{:S(2)}, u32[]{:S(2)}) %collective-permute-start.7) | collective-permute-done | bytes 2097184 | tf_op jit(solution)/shard_map/ppermute | solution.py:15
  392.0 37.3 %collective-permute-done.8 = f32[128,2,2048]{2,0,1:T(8,128)} collective-permute-done((f32[128,2,2048]{2,0,1:T(8,128)}, f32[128,2,2048]{2,0,1:T(8,128)}, u32[]{:S(2)}, u32[]{:S(2)}) %collective-permute-start.8) | collective-permute-done | bytes 2097184 | tf_op jit(solution)/shard_map/ppermute | solution.py:15
  431.9 3.6 multiply_reduce_fusion
  437.5 6.2 %collective-permute-done.9 = f32[6,3,2048]{2,0,1:T(8,128)S(1)} collective-permute-done((f32[6,3,2048]{2,0,1:T(8,128)S(1)}, f32[6,3,2048]{2,0,1:T(8,128)S(1)}, u32[]{:S(2)}, u32[]{:S(2)}) %collective-permute-start.9) | collective-permute-done | bytes 147488 | tf_op jit(solution)/shard_map/ppermute | solution.py:15
  449.5 3.7 all-to-all-start.1
  456.3 74.4 %all-reduce.2.cloned.1.call-done = f32[3,7,2048]{2,0,1:T(4,128)} async-done(((f32[3,7,2048]{2,0,1:T(4,128)}), f32[3,7,2048]{2,0,1:T(4,128)}) %all-reduce.2.cloned.1.call-update) | async-done | bytes 172048 | tf_op jit(solution)/shard_map/psum | solution.py:114
  (107 shorter events, 70.5 us)
Async XLA Ops:
  26.2 4.3 copy-start.13
  26.2 24.4 %all-to-all-start = ((bf16[4,2,98304]{2,1,0:T(2,128)(2,1)}), bf16[4,2,98304]{2,1,0:T(2,128)(2,1)S(1)}, u32[]{:S(2)}, u32[]{:S(2)}) async-start(bf16[4,2,98304]{2,1,0:T(2,128)(2,1)} %reshape.158), calls=%async_computation | async-start | bytes 3145728 | tf_op jit(solution)/shard_map/all_to_all | solution.py:25
  68.2 4.3 copy-start.5
  68.2 6.4 %collective-permute-start = (bf16[6,3,2048]{2,0,1:T(8,128)(2,1)S(1)}, bf16[6,3,2048]{2,0,1:T(8,128)(2,1)S(1)}, u32[]{:S(2)}, u32[]{:S(2)}) collective-permute-start(bf16[6,3,2048]{2,0,1:T(8,128)(2,1)S(1)} %slice.138), channel_id=1, source_target_pairs={{0,4},{4,8},{8,12},{12,16},{16,20},{20,24},{24,28},{1,5},{5,9},{9,... | collective-permute-start | bytes 221192 | tf_op jit(solution)/shard_map/ppermute | solution.py:15
  72.5 6.7 %copy-start.11 = (f32[3,1,2048]{2,0,1:T(4,128)}, f32[3,1,2048]{2,0,1:T(4,128)S(1)}, u32[]{:S(2)}) copy-start(f32[3,1,2048]{2,0,1:T(4,128)S(1)} %copy.107) | copy-start | bytes 73732
  79.2 1.1 copy-start.6
  80.4 57.7 %copy-start.17 = (s32[8]{0:T(128)S(1)}, s32[8]{0:T(128)}, u32[]{:S(2)}) copy-start(s32[8]{0:T(128)} %param.6) | copy-start | bytes 100
  81.5 25.4 %collective-permute-start.1 = (bf16[128,2,2048]{2,0,1:T(8,128)(2,1)S(1)}, bf16[128,2,2048]{2,0,1:T(8,128)(2,1)}, u32[]{:S(2)}, u32[]{:S(2)}) collective-permute-start(bf16[128,2,2048]{2,0,1:T(8,128)(2,1)S(1)} %get-tuple-element.24), channel_id=1, source_target_pairs={{0,4},{4,8},{8,12},{12,16},{16,20},{20,24},{24,28},{1,5},{5,9},{9,... | collective-permute-start | bytes 3145736 | tf_op jit(solution)/shard_map/ppermute | solution.py:15
  106.8 24.9 %collective-permute-start.2 = (bf16[128,2,2048]{2,0,1:T(8,128)(2,1)}, bf16[128,2,2048]{2,0,1:T(8,128)(2,1)}, u32[]{:S(2)}, u32[]{:S(2)}) collective-permute-start(bf16[128,2,2048]{2,0,1:T(8,128)(2,1)} %collective-permute-done.1), channel_id=1, source_target_pairs={{0,4},{4,8},{8,12},{12,16},{16,20},{20,24},{24,28},{1,5},{5,9},{9,... | collective-permute-start | bytes 3145736 | tf_op jit(solution)/shard_map/ppermute | solution.py:15
  131.8 24.7 %collective-permute-start.3 = (bf16[128,2,2048]{2,0,1:T(8,128)(2,1)}, bf16[128,2,2048]{2,0,1:T(8,128)(2,1)}, u32[]{:S(2)}, u32[]{:S(2)}) collective-permute-start(bf16[128,2,2048]{2,0,1:T(8,128)(2,1)} %collective-permute-done.2), channel_id=1, source_target_pairs={{0,4},{4,8},{8,12},{12,16},{16,20},{20,24},{24,28},{1,5},{5,9},{9,... | collective-permute-start | bytes 3145736 | tf_op jit(solution)/shard_map/ppermute | solution.py:15
  156.5 23.9 %collective-permute-start.4 = (bf16[128,2,2048]{2,0,1:T(8,128)(2,1)}, bf16[128,2,2048]{2,0,1:T(8,128)(2,1)}, u32[]{:S(2)}, u32[]{:S(2)}) collective-permute-start(bf16[128,2,2048]{2,0,1:T(8,128)(2,1)} %collective-permute-done.3), channel_id=1, source_target_pairs={{0,4},{4,8},{8,12},{12,16},{16,20},{20,24},{24,28},{1,5},{5,9},{9,... | collective-permute-start | bytes 3145736 | tf_op jit(solution)/shard_map/ppermute | solution.py:15
  203.8 4.1 copy-start.4
  203.8 5.0 copy-start.7
  203.8 5.0 copy-start.9
  245.7 48.1 %slice-start = ((s8[5242880]{0:T(1024)(128)(4,1)}), s8[4194304]{0:T(1024)(128)(4,1)S(1)}, s32[]{:S(2)}) async-start(s8[5242880]{0:T(1024)(128)(4,1)} %bitcast.108), calls=%async_computation.3 | async-start | bytes 8388608
  245.7 48.1 %slice-start.1 = ((s8[5242880]{0:T(1024)(128)(4,1)}), s8[1048576]{0:T(1024)(128)(4,1)S(1)}, s32[]{:S(2)}) async-start(s8[5242880]{0:T(1024)(128)(4,1)} %bitcast.108), calls=%async_computation.4 | async-start | bytes 2097152
  245.7 48.1 %copy-start = (f32[5,128,1,2048]{3,1,2,0:T(8,128)S(1)}, f32[5,128,1,2048]{3,1,2,0:T(8,128)}, u32[]{:S(2)}) copy-start(f32[5,128,1,2048]{3,1,2,0:T(8,128)} %copy.73) | copy-start | bytes 15728644
  247.5 46.3 %collective-permute-start.5 = (f32[128,2,2048]{2,0,1:T(8,128)S(1)}, f32[128,2,2048]{2,0,1:T(8,128)S(1)}, u32[]{:S(2)}, u32[]{:S(2)}) collective-permute-start(f32[128,2,2048]{2,0,1:T(8,128)S(1)} %fusion.25), channel_id=1, source_target_pairs={{4,0},{8,4},{12,8},{16,12},{20,16},{24,20},{28,24},{5,1},{9,5},{13... | collective-permute-start | bytes 6291464 | tf_op jit(solution)/shard_map/ppermute | solution.py:15
  294.2 45.6 %collective-permute-start.6 = (f32[128,2,2048]{2,0,1:T(8,128)S(1)}, f32[128,2,2048]{2,0,1:T(8,128)S(1)}, u32[]{:S(2)}, u32[]{:S(2)}) collective-permute-start(f32[128,2,2048]{2,0,1:T(8,128)S(1)} %fusion.28), channel_id=1, source_target_pairs={{4,0},{8,4},{12,8},{16,12},{20,16},{24,20},{28,24},{5,1},{9,5},{13... | collective-permute-start | bytes 6291464 | tf_op jit(solution)/shard_map/ppermute | solution.py:15
  340.1 47.3 %copy-start.2 = (bf16[640,1,2048]{0,2,1:T(8,128)(2,1)S(1)}, bf16[640,1,2048]{0,2,1:T(8,128)(2,1)}, u32[]{:S(2)}) copy-start(bf16[640,1,2048]{0,2,1:T(8,128)(2,1)} %copy.62) | copy-start | bytes 7864324
  340.1 47.3 %copy-start.3 = (bf16[16,128,640]{2,1,0:T(8,128)(2,1)S(1)}, bf16[16,128,640]{2,1,0:T(8,128)(2,1)}, u32[]{:S(2)}) copy-start(bf16[16,128,640]{2,1,0:T(8,128)(2,1)} %fusion.2) | copy-start | bytes 7864324
  340.1 44.4 %collective-permute-start.7 = (f32[128,2,2048]{2,0,1:T(8,128)S(1)}, f32[128,2,2048]{2,0,1:T(8,128)S(1)}, u32[]{:S(2)}, u32[]{:S(2)}) collective-permute-start(f32[128,2,2048]{2,0,1:T(8,128)S(1)} %fusion.31), channel_id=1, source_target_pairs={{4,0},{8,4},{12,8},{16,12},{20,16},{24,20},{28,24},{5,1},{9,5},{13... | collective-permute-start | bytes 6291464 | tf_op jit(solution)/shard_map/ppermute | solution.py:15
  386.1 43.2 %collective-permute-start.8 = (f32[128,2,2048]{2,0,1:T(8,128)}, f32[128,2,2048]{2,0,1:T(8,128)}, u32[]{:S(2)}, u32[]{:S(2)}) collective-permute-start(f32[128,2,2048]{2,0,1:T(8,128)} %fusion.23), channel_id=1, source_target_pairs={{4,0},{8,4},{12,8},{16,12},{20,16},{24,20},{28,24},{5,1},{9,5},{13... | collective-permute-start | bytes 6291464 | tf_op jit(solution)/shard_map/ppermute | solution.py:15
  392.0 39.8 %copy-start.1 = (f32[128,1,2048]{2,0,1:T(8,128)S(1)}, f32[128,1,2048]{2,0,1:T(8,128)}, u32[]{:S(2)}) copy-start(f32[128,1,2048]{2,0,1:T(8,128)} %copy.75) | copy-start | bytes 3145732
  435.5 8.3 %collective-permute-start.9 = (f32[6,3,2048]{2,0,1:T(8,128)S(1)}, f32[6,3,2048]{2,0,1:T(8,128)S(1)}, u32[]{:S(2)}, u32[]{:S(2)}) collective-permute-start(f32[6,3,2048]{2,0,1:T(8,128)S(1)} %fusion.45), channel_id=1, source_target_pairs={{4,0},{8,4},{12,8},{16,12},{20,16},{24,20},{28,24},{5,1},{9,5},{13... | collective-permute-start | bytes 442376 | tf_op jit(solution)/shard_map/ppermute | solution.py:15
  437.5 6.6 %copy-start.12 = (f32[3,1,2048]{2,0,1:T(4,128)S(1)}, f32[3,1,2048]{2,0,1:T(4,128)}, u32[]{:S(2)}) copy-start(f32[3,1,2048]{2,0,1:T(4,128)} %copy-done.11) | copy-start | bytes 73732
  446.8 6.5 %copy-start.16 = (f32[3,2048]{1,0:T(4,128)S(1)}, f32[3,2048]{1,0:T(4,128)}, u32[]{:S(2)}) copy-start(f32[3,2048]{1,0:T(4,128)} %get-tuple-element.17) | copy-start | bytes 73732
  446.8 7.2 %copy-start.15 = (f32[3,2048]{1,0:T(4,128)S(1)}, f32[3,2048]{1,0:T(4,128)}, u32[]{:S(2)}) copy-start(f32[3,2048]{1,0:T(4,128)} %get-tuple-element.16) | copy-start | bytes 73732
  446.8 7.8 %copy-start.14 = (f32[3,2048]{1,0:T(4,128)S(1)}, f32[3,2048]{1,0:T(4,128)}, u32[]{:S(2)}) copy-start(f32[3,2048]{1,0:T(4,128)} %get-tuple-element.15) | copy-start | bytes 73732
  449.5 5.7 %copy-start.8 = (bf16[128,16,128]{0,2,1:T(8,128)(2,1)S(1)}, bf16[128,16,128]{0,2,1:T(8,128)(2,1)}, u32[]{:S(2)}) copy-start(bf16[128,16,128]{0,2,1:T(8,128)(2,1)} %get-tuple-element.41) | copy-start | bytes 1572868
  449.5 82.8 %all-to-all-start.1 = ((bf16[128,3,2048]{2,1,0:T(4,128)(2,1)}), bf16[128,3,2048]{2,1,0:T(4,128)(2,1)S(1)}, u32[]{:S(2)}, u32[]{:S(2)}) async-start(bf16[128,3,2048]{2,1,0:T(4,128)(2,1)} %copy.76), calls=%async_computation.1 | async-start | bytes 4194304 | tf_op jit(solution)/shard_map/all_to_all | solution.py:115
  453.3 77.4 %all-reduce.2.cloned.1.call-start = ((), (), s32[]{:S(2)}) async-start(), calls=%async_computation.2 | async-start | bytes 458752 | tf_op jit(solution)/shard_map/psum | solution.py:114
  (1 other events, 0.7 us)
Sparse Core Ops, SparseCore 0:
  458.1 72.5 all-reduce.1
where the time goes:
time: 544 us; the launch traced here: 542 us
  waiting for transfers between devices  328 us (60%)
  local copies, waits for them, and re-layouts  114 us (21%)
  starting transfers between devices  42.9 us (8%)
  matrix products  22.2 us (4%)
  other arithmetic  20.2 us (4%)
  between operations  14.5 us (3%)
    ppermute x10, waiting for transfers between devices, from_behind(): lax.ppermute(value, axis, [(source, source + steps) for source in range(f...  234 us
    psum x1, waiting for transfers between devices, shards(): filter_grad = lax.psum(tap_terms, 'ctx')  74.4 us
    unnamed x63, local copies, waits for them, and re-layouts  44.5 us
    ppermute x10, starting transfers between devices, from_behind(): lax.ppermute(value, axis, [(source, source + steps) for source in range(f...  34.8 us
    another operation x3, local copies, waits for them, and re-layouts, shards(): jnp.stack([key_part.reshape(reach, tokens, width), value_part.reshape(rea...  22 us
    all_to_all x1, waiting for transfers between devices, shards(): local = lax.all_to_all(qkv, 'tp', split_axis=2, concat_axis=0, tiled=True)  19.9 us
  transfers between devices with their start and end apart: 13, of which 12 were waited for; matrix products, arithmetic and copies ran while one was open for 5% of the time, Pallas kernels for 0%

commit v1 on v0

--- a/solution.py
+++ b/solution.py
@@ -2,6 +2,7 @@
 import jax.numpy as jnp
 from jax import lax
 from jax.sharding import PartitionSpec as P
+from jax.lax import all_gather
 
 HEAD_DIM = 128
 KW = 7
@@ -111,7 +112,8 @@
         ],
         axis=1,
     )
-    filter_grad = lax.psum(tap_terms, "ctx")
+    view_yards_for = lambda w_in, mesh_ax: all_gather(w_in, mesh_ax).sum(axis=0)
+    filter_grad = view_yards_for(tap_terms, "ctx")
     qkv_grad = lax.all_to_all(
         input_grad.astype(jnp.bfloat16), "tp", split_axis=0, concat_axis=2, tiled=True
     )

time: 544 us -> 498 us (0.915)
  waiting for transfers between devices: 328 us -> 282 us
    psum x1 -> x0, waiting for transfers between devices: 74.4 us -> none  [shards(): filter_grad = lax.psum(tap_terms, 'ctx')]
    all_to_all x1, waiting for transfers between devices: 0.01 us -> 24.6 us  [shards(): lax.all_to_all(input_grad.astype(jnp.bfloat16), 'tp', split_axis=0, conca...]
    all_gather x0 -> x1, waiting for transfers between devices: none -> 6.76 us  [shards(): view_yards_for = lambda w_in, mesh_ax: all_gather(w_in, mesh_ax).sum(axis=0)]
    unnamed x63 -> x54, local copies, waits for them, and re-layouts: 44.5 us -> 40.7 us
  transfers between devices with their start and end apart: 13 -> 13, of which waited for: 12 -> 13; matrix products, arithmetic and copies ran while one was open for 5% -> 8% of each run, Pallas kernels for 0% -> 0%
where the time goes in v1:
time: 498 us; the launch traced here: 496 us
  waiting for transfers between devices  282 us (57%)
  local copies, waits for them, and re-layouts  111 us (22%)
  starting transfers between devices  42.7 us (9%)
  other arithmetic  24.5 us (5%)
  matrix products  22.2 us (4%)
  between operations  14.5 us (3%)
    ppermute x10, waiting for transfers between devices, from_behind(): lax.ppermute(value, axis, [(source, source + steps) for source in range(f...  230 us
    unnamed x54, local copies, waits for them, and re-layouts  40.7 us
    ppermute x10, starting transfers between devices, from_behind(): lax.ppermute(value, axis, [(source, source + steps) for source in range(f...  34.8 us
    all_to_all x1, waiting for transfers between devices, shards(): lax.all_to_all(input_grad.astype(jnp.bfloat16), 'tp', split_axis=0, conca...  24.6 us
    another operation x3, local copies, waits for them, and re-layouts, shards(): jnp.stack([key_part.reshape(reach, tokens, width), value_part.reshape(rea...  22 us
    all_to_all x1, waiting for transfers between devices, shards(): local = lax.all_to_all(qkv, 'tp', split_axis=2, concat_axis=0, tiled=True)  19.9 us
    all_to_all x1, local copies, waits for them, and re-layouts, shards(): local = lax.all_to_all(qkv, 'tp', split_axis=2, concat_axis=0, tiled=True)  10.5 us
    slice x2, local copies, waits for them, and re-layouts, shards(): keys = joined[:, 0].reshape(reach * tokens, heads, HEAD_DIM)  10.1 us
  transfers between devices with their start and end apart: 13, of which 13 were waited for; matrix products, arithmetic and copies ran while one was open for 8% of the time, Pallas kernels for 0%

profile of v1, /device:TPU:0, one launch (start us, length us, event | category | flops | bytes accessed | tf_op | source)
XLA Modules:
  0.0 496.3 jit_solution(9346955197506745826)
XLA Ops:
  7.2 10.7 %copy.55 = bf16[32,3,8192]{0,1,2:T(4,128)(2,1)} copy(bf16[32,3,8192]{2,0,1:T(8,128)(2,1)} %param.4) | data formatting | bytes 3145728 | tf_op args[0]
  17.8 8.4 %reshape.159 = bf16[4,2,98304]{2,1,0:T(2,128)(2,1)} reshape(bf16[8192,3,32]{2,1,0:T(4,128)(2,1)} %bitcast.101) | data formatting | bytes 3145728
  26.2 4.3 all-to-all-start
  30.7 19.9 %all-to-all-done = bf16[4,2,98304]{2,1,0:T(2,128)(2,1)S(1)} async-done(((bf16[4,2,98304]{2,1,0:T(2,128)(2,1)}), bf16[4,2,98304]{2,1,0:T(2,128)(2,1)S(1)}, u32[]{:S(2)}, u32[]{:S(2)}) %all-to-all-start) | async-done | bytes 1572896 | tf_op jit(solution)/shard_map/all_to_all | solution.py:26
  50.6 7.1 %reshape.160 = bf16[8192,3,32]{2,1,0:T(4,128)(2,1)} reshape(bf16[4,2,98304]{2,1,0:T(2,128)(2,1)S(1)} %all-to-all-done) | data formatting | bytes 3145728
  57.7 10.5 %copy.57 = bf16[4,32,3,2048]{3,1,0,2:T(8,128)(2,1)S(1)} copy(bf16[4,32,3,2048]{1,2,3,0:T(4,128)(2,1)} %bitcast.100) | data formatting | bytes 3145728 | tf_op jit(solution)/shard_map/all_to_all | solution.py:26
  68.3 4.2 collective-permute-start
  81.5 5.3 %collective-permute-start.1 = (bf16[128,2,2048]{2,0,1:T(8,128)(2,1)S(1)}, bf16[128,2,2048]{2,0,1:T(8,128)(2,1)}, u32[]{:S(2)}, u32[]{:S(2)}) collective-permute-start(bf16[128,2,2048]{2,0,1:T(8,128)(2,1)S(1)} %get-tuple-element.24), channel_id=1, source_target_pairs={{0,4},{4,8},{8,12},{12,16},{16,20},{20,24},{24,28},{1,5},{5,9},{9,... | collective-permute-start | bytes 3145736 | tf_op jit(solution)/shard_map/ppermute | solution.py:16
  86.9 20.0 %collective-permute-done.1 = bf16[128,2,2048]{2,0,1:T(8,128)(2,1)} collective-permute-done((bf16[128,2,2048]{2,0,1:T(8,128)(2,1)S(1)}, bf16[128,2,2048]{2,0,1:T(8,128)(2,1)}, u32[]{:S(2)}, u32[]{:S(2)}) %collective-permute-start.1) | collective-permute-done | bytes 1048608 | tf_op jit(solution)/shard_map/ppermute | solution.py:16
  106.9 5.5 %collective-permute-start.2 = (bf16[128,2,2048]{2,0,1:T(8,128)(2,1)}, bf16[128,2,2048]{2,0,1:T(8,128)(2,1)}, u32[]{:S(2)}, u32[]{:S(2)}) collective-permute-start(bf16[128,2,2048]{2,0,1:T(8,128)(2,1)} %collective-permute-done.1), channel_id=1, source_target_pairs={{0,4},{4,8},{8,12},{12,16},{16,20},{20,24},{24,28},{1,5},{5,9},{9,... | collective-permute-start | bytes 3145736 | tf_op jit(solution)/shard_map/ppermute | solution.py:16
  112.9 18.9 %collective-permute-done.2 = bf16[128,2,2048]{2,0,1:T(8,128)(2,1)} collective-permute-done((bf16[128,2,2048]{2,0,1:T(8,128)(2,1)}, bf16[128,2,2048]{2,0,1:T(8,128)(2,1)}, u32[]{:S(2)}, u32[]{:S(2)}) %collective-permute-start.2) | collective-permute-done | bytes 1048608 | tf_op jit(solution)/shard_map/ppermute | solution.py:16
  131.8 6.2 %collective-permute-start.3 = (bf16[128,2,2048]{2,0,1:T(8,128)(2,1)}, bf16[128,2,2048]{2,0,1:T(8,128)(2,1)}, u32[]{:S(2)}, u32[]{:S(2)}) collective-permute-start(bf16[128,2,2048]{2,0,1:T(8,128)(2,1)} %collective-permute-done.2), channel_id=1, source_target_pairs={{0,4},{4,8},{8,12},{12,16},{16,20},{20,24},{24,28},{1,5},{5,9},{9,... | collective-permute-start | bytes 3145736 | tf_op jit(solution)/shard_map/ppermute | solution.py:16
  141.8 14.8 %collective-permute-done.3 = bf16[128,2,2048]{2,0,1:T(8,128)(2,1)} collective-permute-done((bf16[128,2,2048]{2,0,1:T(8,128)(2,1)}, bf16[128,2,2048]{2,0,1:T(8,128)(2,1)}, u32[]{:S(2)}, u32[]{:S(2)}) %collective-permute-start.3) | collective-permute-done | bytes 1048608 | tf_op jit(solution)/shard_map/ppermute | solution.py:16
  156.5 6.3 %collective-permute-start.4 = (bf16[128,2,2048]{2,0,1:T(8,128)(2,1)}, bf16[128,2,2048]{2,0,1:T(8,128)(2,1)}, u32[]{:S(2)}, u32[]{:S(2)}) collective-permute-start(bf16[128,2,2048]{2,0,1:T(8,128)(2,1)} %collective-permute-done.3), channel_id=1, source_target_pairs={{0,4},{4,8},{8,12},{12,16},{16,20},{20,24},{24,28},{1,5},{5,9},{9,... | collective-permute-start | bytes 3145736 | tf_op jit(solution)/shard_map/ppermute | solution.py:16
  182.7 5.7 %fusion.48 = (bf16[640,1,2048]{2,0,1:T(8,128)(2,1)}, bf16[640,1,2048]{2,0,1:T(8,128)(2,1)}) fusion(bf16[640,2,2048]{2,0,1:T(8,128)(2,1)} %constant_dynamic-update-slice_fusion), kind=kLoop, calls=%fused_computation.99 | loop fusion | bytes 10485760 | tf_op jit(solution)/shard_map/slice | solution.py:48
  188.4 4.4 copy.60
  192.8 4.5 copy.58
  197.2 6.6 %fusion.52 = (f32[16,128]{1,0:T(8,128)S(1)}, f32[16,128,640]{2,1,0:T(8,128)}) fusion(pred[128,640]{1,0:T(8,128)(4,1)} %and_and_fusion, bf16[128,16,128]{0,2,1:T(8,128)(2,1)} %bitcast.111, bf16[640,16,128]{0,2,1:T(8,128)(2,1)} %bitcast.102), kind=kOutput, calls=%fused_computation.103 | convolution fusion | flops 342098560 | bytes 8478720 | tf_op jit(solution)/shard_map/sub | solution.py:72
  203.8 4.1 fusion.18
  213.3 5.3 %copy.70 = f32[640,16,128]{2,1,0:T(8,128)} copy(f32[640,16,128]{2,0,1:T(8,128)S(1)} %fusion.18) | data formatting | bytes 10485760 | tf_op jit(solution)/shard_map/hqk,qhd->khd/transpose | solution.py:81
  218.7 6.8 %stack_reshape.7 = f32[5,128,1,2048]{3,1,0,2:T(8,128)} reshape(f32[640,16,128]{2,1,0:T(8,128)} %copy.70) | data formatting | bytes 10485760 | tf_op jit(solution)/shard_map/stack;reshape | solution.py:96
  225.5 5.0 %convolution_bitcast_fusion = f32[640,16,128]{0,2,1:T(8,128)} fusion(bf16[128,16,128]{0,2,1:T(8,128)(2,1)} %bitcast.112, bf16[16,128,640]{2,1,0:T(8,128)(2,1)} %fusion.2), kind=kOutput, calls=%fused_computation.48 | convolution fusion | flops 335544320 | bytes 8388608 | tf_op jit(solution)/shard_map/hqk,qhd->khd/dot_general | solution.py:93
  230.5 7.4 %reshape.153 = f32[5,128,1,2048]{1,0,3,2:T(8,128)} reshape(f32[640,16,128]{0,2,1:T(8,128)} %convolution_bitcast_fusion) | data formatting | bytes 10485760 | tf_op jit(solution)/shard_map/stack;reshape | solution.py:96
  237.8 7.8 %copy.71 = f32[5,128,1,2048]{3,1,2,0:T(8,128)} copy(f32[5,128,1,2048]{1,0,3,2:T(8,128)} %reshape.153) | data formatting | bytes 10485760 | tf_op jit(solution)/shard_map/stack;reshape | solution.py:96
  249.1 44.7 %collective-permute-done.5 = f32[128,2,2048]{2,0,1:T(8,128)S(1)} collective-permute-done((f32[128,2,2048]{2,0,1:T(8,128)S(1)}, f32[128,2,2048]{2,0,1:T(8,128)S(1)}, u32[]{:S(2)}, u32[]{:S(2)}) %collective-permute-start.5) | collective-permute-done | bytes 2097184 | tf_op jit(solution)/shard_map/ppermute | solution.py:16
  295.6 44.1 %collective-permute-done.6 = f32[128,2,2048]{2,0,1:T(8,128)S(1)} collective-permute-done((f32[128,2,2048]{2,0,1:T(8,128)S(1)}, f32[128,2,2048]{2,0,1:T(8,128)S(1)}, u32[]{:S(2)}, u32[]{:S(2)}) %collective-permute-start.6) | collective-permute-done | bytes 2097184 | tf_op jit(solution)/shard_map/ppermute | solution.py:16
  341.7 42.9 %collective-permute-done.7 = f32[128,2,2048]{2,0,1:T(8,128)S(1)} collective-permute-done((f32[128,2,2048]{2,0,1:T(8,128)S(1)}, f32[128,2,2048]{2,0,1:T(8,128)S(1)}, u32[]{:S(2)}, u32[]{:S(2)}) %collective-permute-start.7) | collective-permute-done | bytes 2097184 | tf_op jit(solution)/shard_map/ppermute | solution.py:16
  392.0 37.3 %collective-permute-done.8 = f32[128,2,2048]{2,0,1:T(8,128)} collective-permute-done((f32[128,2,2048]{2,0,1:T(8,128)}, f32[128,2,2048]{2,0,1:T(8,128)}, u32[]{:S(2)}, u32[]{:S(2)}) %collective-permute-start.8) | collective-permute-done | bytes 2097184 | tf_op jit(solution)/shard_map/ppermute | solution.py:16
  438.1 3.1 collective-permute-done.9
  448.8 3.6 all-to-all-start.1
  453.4 24.6 %all-to-all-done.1 = bf16[128,3,2048]{2,1,0:T(4,128)(2,1)S(1)} async-done(((bf16[128,3,2048]{2,1,0:T(4,128)(2,1)}), bf16[128,3,2048]{2,1,0:T(4,128)(2,1)S(1)}, u32[]{:S(2)}, u32[]{:S(2)}) %all-to-all-start.1) | async-done | bytes 1572896 | tf_op jit(solution)/shard_map/all_to_all | solution.py:117
  480.5 6.8 %all-gather.3.cloned.1.call-done = f32[24,7,2048]{2,1,0:T(8,128)} async-done(((f32[3,7,2048]{2,1,0:T(8,128)}), f32[24,7,2048]{2,1,0:T(8,128)}) %all-gather.3.cloned.1.call-update) | async-done | bytes 1376272 | tf_op jit(solution)/shard_map/all_gather | solution.py:115
  (106 shorter events, 75.0 us)
Async XLA Ops:
  26.2 4.3 copy-start.15
  26.2 24.4 %all-to-all-start = ((bf16[4,2,98304]{2,1,0:T(2,128)(2,1)}), bf16[4,2,98304]{2,1,0:T(2,128)(2,1)S(1)}, u32[]{:S(2)}, u32[]{:S(2)}) async-start(bf16[4,2,98304]{2,1,0:T(2,128)(2,1)} %reshape.159), calls=%async_computation | async-start | bytes 3145728 | tf_op jit(solution)/shard_map/all_to_all | solution.py:26
  30.5 456.7 %all-gather.3.cloned.1.call-start = ((), (), s32[]{:S(2)}) async-start(), calls=%async_computation.2 | async-start | bytes 1769472 | tf_op jit(solution)/shard_map/all_gather | solution.py:115
  68.2 4.3 copy-start.8
  68.3 6.4 %collective-permute-start = (bf16[6,3,2048]{2,0,1:T(8,128)(2,1)S(1)}, bf16[6,3,2048]{2,0,1:T(8,128)(2,1)S(1)}, u32[]{:S(2)}, u32[]{:S(2)}) collective-permute-start(bf16[6,3,2048]{2,0,1:T(8,128)(2,1)S(1)} %slice.138), channel_id=1, source_target_pairs={{0,4},{4,8},{8,12},{12,16},{16,20},{20,24},{24,28},{1,5},{5,9},{9,... | collective-permute-start | bytes 221192 | tf_op jit(solution)/shard_map/ppermute | solution.py:16
  72.5 6.7 %copy-start.13 = (f32[3,1,2048]{2,0,1:T(4,128)}, f32[3,1,2048]{2,0,1:T(4,128)S(1)}, u32[]{:S(2)}) copy-start(f32[3,1,2048]{2,0,1:T(4,128)S(1)} %copy.104) | copy-start | bytes 73732
  79.2 1.1 copy-start.9
  80.4 57.7 %copy-start.16 = (s32[8]{0:T(128)S(1)}, s32[8]{0:T(128)}, u32[]{:S(2)}) copy-start(s32[8]{0:T(128)} %param.6) | copy-start | bytes 100
  81.5 25.4 %collective-permute-start.1 = (bf16[128,2,2048]{2,0,1:T(8,128)(2,1)S(1)}, bf16[128,2,2048]{2,0,1:T(8,128)(2,1)}, u32[]{:S(2)}, u32[]{:S(2)}) collective-permute-start(bf16[128,2,2048]{2,0,1:T(8,128)(2,1)S(1)} %get-tuple-element.24), channel_id=1, source_target_pairs={{0,4},{4,8},{8,12},{12,16},{16,20},{20,24},{24,28},{1,5},{5,9},{9,... | collective-permute-start | bytes 3145736 | tf_op jit(solution)/shard_map/ppermute | solution.py:16
  106.9 24.9 %collective-permute-start.2 = (bf16[128,2,2048]{2,0,1:T(8,128)(2,1)}, bf16[128,2,2048]{2,0,1:T(8,128)(2,1)}, u32[]{:S(2)}, u32[]{:S(2)}) collective-permute-start(bf16[128,2,2048]{2,0,1:T(8,128)(2,1)} %collective-permute-done.1), channel_id=1, source_target_pairs={{0,4},{4,8},{8,12},{12,16},{16,20},{20,24},{24,28},{1,5},{5,9},{9,... | collective-permute-start | bytes 3145736 | tf_op jit(solution)/shard_map/ppermute | solution.py:16
  131.8 24.7 %collective-permute-start.3 = (bf16[128,2,2048]{2,0,1:T(8,128)(2,1)}, bf16[128,2,2048]{2,0,1:T(8,128)(2,1)}, u32[]{:S(2)}, u32[]{:S(2)}) collective-permute-start(bf16[128,2,2048]{2,0,1:T(8,128)(2,1)} %collective-permute-done.2), channel_id=1, source_target_pairs={{0,4},{4,8},{8,12},{12,16},{16,20},{20,24},{24,28},{1,5},{5,9},{9,... | collective-permute-start | bytes 3145736 | tf_op jit(solution)/shard_map/ppermute | solution.py:16
  156.5 23.9 %collective-permute-start.4 = (bf16[128,2,2048]{2,0,1:T(8,128)(2,1)}, bf16[128,2,2048]{2,0,1:T(8,128)(2,1)}, u32[]{:S(2)}, u32[]{:S(2)}) collective-permute-start(bf16[128,2,2048]{2,0,1:T(8,128)(2,1)} %collective-permute-done.3), channel_id=1, source_target_pairs={{0,4},{4,8},{8,12},{12,16},{16,20},{20,24},{24,28},{1,5},{5,9},{9,... | collective-permute-start | bytes 3145736 | tf_op jit(solution)/shard_map/ppermute | solution.py:16
  203.8 4.1 copy-start.7
  203.8 5.0 %copy-start.10 = (f32[16,128,640]{2,1,0:T(8,128)S(1)}, f32[16,128,640]{2,1,0:T(8,128)}, u32[]{:S(2)}) copy-start(f32[16,128,640]{2,1,0:T(8,128)} %get-tuple-element.39) | copy-start | bytes 15728644
  203.8 5.0 %copy-start.12 = (bf16[128,2048]{0,1:T(8,128)(2,1)S(1)}, bf16[128,2048]{0,1:T(8,128)(2,1)}, u32[]{:S(2)}) copy-start(bf16[128,2048]{0,1:T(8,128)(2,1)} %copy.63) | copy-start | bytes 1572868
  245.7 48.1 %slice-start = ((s8[5242880]{0:T(1024)(128)(4,1)}), s8[4194304]{0:T(1024)(128)(4,1)S(1)}, s32[]{:S(2)}) async-start(s8[5242880]{0:T(1024)(128)(4,1)} %bitcast.95), calls=%async_computation.3 | async-start | bytes 8388608
  245.7 48.1 %slice-start.1 = ((s8[5242880]{0:T(1024)(128)(4,1)}), s8[1048576]{0:T(1024)(128)(4,1)S(1)}, s32[]{:S(2)}) async-start(s8[5242880]{0:T(1024)(128)(4,1)} %bitcast.95), calls=%async_computation.4 | async-start | bytes 2097152
  245.7 48.1 %copy-start = (f32[5,128,1,2048]{3,1,2,0:T(8,128)S(1)}, f32[5,128,1,2048]{3,1,2,0:T(8,128)}, u32[]{:S(2)}) copy-start(f32[5,128,1,2048]{3,1,2,0:T(8,128)} %copy.71) | copy-start | bytes 15728644
  247.5 46.3 %collective-permute-start.5 = (f32[128,2,2048]{2,0,1:T(8,128)S(1)}, f32[128,2,2048]{2,0,1:T(8,128)S(1)}, u32[]{:S(2)}, u32[]{:S(2)}) collective-permute-start(f32[128,2,2048]{2,0,1:T(8,128)S(1)} %fusion.25), channel_id=1, source_target_pairs={{4,0},{8,4},{12,8},{16,12},{20,16},{24,20},{28,24},{5,1},{9,5},{13... | collective-permute-start | bytes 6291464 | tf_op jit(solution)/shard_map/ppermute | solution.py:16
  294.1 45.6 %collective-permute-start.6 = (f32[128,2,2048]{2,0,1:T(8,128)S(1)}, f32[128,2,2048]{2,0,1:T(8,128)S(1)}, u32[]{:S(2)}, u32[]{:S(2)}) collective-permute-start(f32[128,2,2048]{2,0,1:T(8,128)S(1)} %fusion.28), channel_id=1, source_target_pairs={{4,0},{8,4},{12,8},{16,12},{20,16},{24,20},{28,24},{5,1},{9,5},{13... | collective-permute-start | bytes 6291464 | tf_op jit(solution)/shard_map/ppermute | solution.py:16
  340.1 47.3 %copy-start.5 = (bf16[640,1,2048]{0,2,1:T(8,128)(2,1)S(1)}, bf16[640,1,2048]{0,2,1:T(8,128)(2,1)}, u32[]{:S(2)}) copy-start(bf16[640,1,2048]{0,2,1:T(8,128)(2,1)} %copy.60) | copy-start | bytes 7864324
  340.1 47.3 %copy-start.6 = (bf16[16,128,640]{2,1,0:T(8,128)(2,1)S(1)}, bf16[16,128,640]{2,1,0:T(8,128)(2,1)}, u32[]{:S(2)}) copy-start(bf16[16,128,640]{2,1,0:T(8,128)(2,1)} %fusion.2) | copy-start | bytes 7864324
  340.1 44.4 %collective-permute-start.7 = (f32[128,2,2048]{2,0,1:T(8,128)S(1)}, f32[128,2,2048]{2,0,1:T(8,128)S(1)}, u32[]{:S(2)}, u32[]{:S(2)}) collective-permute-start(f32[128,2,2048]{2,0,1:T(8,128)S(1)} %fusion.31), channel_id=1, source_target_pairs={{4,0},{8,4},{12,8},{16,12},{20,16},{24,20},{28,24},{5,1},{9,5},{13... | collective-permute-start | bytes 6291464 | tf_op jit(solution)/shard_map/ppermute | solution.py:16
  386.1 43.2 %collective-permute-start.8 = (f32[128,2,2048]{2,0,1:T(8,128)}, f32[128,2,2048]{2,0,1:T(8,128)}, u32[]{:S(2)}, u32[]{:S(2)}) collective-permute-start(f32[128,2,2048]{2,0,1:T(8,128)} %fusion.23), channel_id=1, source_target_pairs={{4,0},{8,4},{12,8},{16,12},{20,16},{24,20},{28,24},{5,1},{9,5},{13... | collective-permute-start | bytes 6291464 | tf_op jit(solution)/shard_map/ppermute | solution.py:16
  392.0 39.8 %copy-start.3 = (f32[128,1,2048]{2,0,1:T(8,128)S(1)}, f32[128,1,2048]{2,0,1:T(8,128)}, u32[]{:S(2)}) copy-start(f32[128,1,2048]{2,0,1:T(8,128)} %copy.73) | copy-start | bytes 3145732
  431.8 5.1 %copy-start.1 = (f32[128,2,2048]{2,0,1:T(8,128)}, f32[128,2,2048]{2,0,1:T(8,128)S(1)}, u32[]{:S(2)}) copy-start(f32[128,2,2048]{2,0,1:T(8,128)S(1)} %fusion.33) | copy-start | bytes 6291460
  432.6 8.6 %collective-permute-start.9 = (f32[6,3,2048]{2,0,1:T(8,128)}, f32[6,3,2048]{2,0,1:T(8,128)}, u32[]{:S(2)}, u32[]{:S(2)}) collective-permute-start(f32[6,3,2048]{2,0,1:T(8,128)} %fusion.45), channel_id=1, source_target_pairs={{4,0},{8,4},{12,8},{16,12},{20,16},{24,20},{28,24},{5,1},{9,5},{13... | collective-permute-start | bytes 442376 | tf_op jit(solution)/shard_map/ppermute | solution.py:16
  438.1 5.4 %copy-start.2 = (f32[128,2,2048]{2,0,1:T(8,128)S(1)}, f32[128,2,2048]{2,0,1:T(8,128)}, u32[]{:S(2)}) copy-start(f32[128,2,2048]{2,0,1:T(8,128)} %copy-done.1) | copy-start | bytes 6291460
  438.1 5.4 %copy-start.4 = (f32[128,1,2048]{2,0,1:T(8,128)S(1)}, f32[128,1,2048]{2,0,1:T(8,128)}, u32[]{:S(2)}) copy-start(f32[128,1,2048]{2,0,1:T(8,128)} %copy.73) | copy-start | bytes 3145732
  438.1 5.4 %copy-start.14 = (f32[3,1,2048]{2,0,1:T(4,128)S(1)}, f32[3,1,2048]{2,0,1:T(4,128)}, u32[]{:S(2)}) copy-start(f32[3,1,2048]{2,0,1:T(4,128)} %copy-done.13) | copy-start | bytes 73732
  446.1 6.3 %copy-start.11 = (bf16[128,16,128]{0,2,1:T(8,128)(2,1)S(1)}, bf16[128,16,128]{0,2,1:T(8,128)(2,1)}, u32[]{:S(2)}) copy-start(bf16[128,16,128]{0,2,1:T(8,128)(2,1)} %get-tuple-element.41) | copy-start | bytes 1572868
  448.8 29.3 %all-to-all-start.1 = ((bf16[128,3,2048]{2,1,0:T(4,128)(2,1)}), bf16[128,3,2048]{2,1,0:T(4,128)(2,1)S(1)}, u32[]{:S(2)}, u32[]{:S(2)}) async-start(bf16[128,3,2048]{2,1,0:T(4,128)(2,1)} %copy.74), calls=%async_computation.1 | async-start | bytes 4194304 | tf_op jit(solution)/shard_map/all_to_all | solution.py:117
Sparse Core Ops, SparseCore 0:
  438.2 49.0 all-gather.2
